TPU v7x, 512 devices: a whole 4x4x16 slice. The times are simulated.
512 devices in a mesh: space: 128 (over z, x, core), chan: 4 (over y).
Axes of the slice: x: 4, y: 4, z: 16, core: 2. Of those that a mesh axis runs over, the one named last changes fastest.
Arguments:
- features: bfloat16 [1024, 64, 512], P('space', 'chan'), may hold values from -6 to 6
- weight: bfloat16 [27, 64, 64], P(None, 'chan'), may hold values from -0.15625 to 0.15625
- cotangent: bfloat16 [1024, 64, 512], P('space', 'chan'), may hold values from -6 to 6
- neighbours: int32 [1024, 27], P('space'), may hold values from -1 to 1023, as said below
Outputs:
- output: bfloat16 [1024, 64, 512], P('space', 'chan')
- grad_input: bfloat16 [1024, 64, 512], P('space', 'chan')
- grad_weight: float32 [27, 64, 64], P(None, 'chan')
Inputs may be any that keep to these rules, and one draw needn't show every extreme that they name: `neighbours`: row r lists, for the displacement (i, j, k) in the finite set (-1, 0, 1)^3 at entry 9 (i + 1) + 3 (j + 1) + (k + 1), the slot of the brick at that displacement in bricks, or -1 where the scene has none. Slot s belongs to device s // 8 of space, and a neighbour at first displacement i belongs to the device of index one's own + i. The relation is symmetric: if row r names s at entry m, row s names r at entry 26 - m. A device's occupied bricks fill its first slots, and the last device of space has all 8 slots occupied; an empty slot's row is all -1, no row names an empty slot, and an occupied brick's entry 13 is its own slot.
All inputs are finite; a program needn't handle non-finite values.
Results may differ from a plain program's by a relative error of at most 0.001.
Values may be sent and summed in bfloat16 or wider, within the bound.
A program may use at most 128 MiB of HBM per device.

v0:
```python
import jax
import jax.numpy as jnp
import numpy as np
from jax import lax
from jax.sharding import PartitionSpec as P

flat_width = 896
source_width = 1152


def shifted(shard, axis, by):
    length = lax.axis_size(axis)
    pairs = [(i, i + by) for i in range(length) if 0 <= i + by < length]
    return lax.ppermute(shard, axis, pairs)


def axis_pairs(step):
    if step == 0:
        return [(0, 7)]
    if step == 1:
        return [(place + 1, place) for place in range(8)]
    return [(9, 0)]


def piece_tables():
    lists = []
    positions = []
    for step_x in range(3):
        for step_y in range(3):
            for step_z in range(3):
                source_ids = []
                for grid_x, vox_u in axis_pairs(step_x):
                    for grid_y, vox_v in axis_pairs(step_y):
                        for grid_z, vox_w in axis_pairs(step_z):
                            if step_x == 1:
                                source_ids.append(64 * vox_u + 8 * vox_v + vox_w)
                            else:
                                source_ids.append(8 * vox_v + vox_w)
                            positions.append(100 * grid_x + 10 * grid_y + grid_z)
                lists.append(np.array(source_ids, dtype=np.int32))
    order = np.argsort(np.array(positions, dtype=np.int64)).astype(np.int32)
    return (lists, order)


def grid_tables():
    into_grid = np.zeros((flat_width,), dtype=np.int32)
    valid = np.zeros((flat_width,), dtype=np.float32)
    back_ids = np.zeros((512,), dtype=np.int32)
    for vox_u in range(8):
        for vox_v in range(8):
            for vox_w in range(8):
                place = 100 * vox_u + 10 * vox_v + vox_w
                into_grid[place] = 64 * vox_u + 8 * vox_v + vox_w
                valid[place] = 1.0
                back_ids[64 * vox_u + 8 * vox_v + vox_w] = place
    return (into_grid, valid, back_ids)


def split_planes(bricks):
    return (bricks[..., 0:64], bricks[..., 448:512])


def neighbour_planes(bricks):
    previous = shifted(bricks, "space", 1)
    following = shifted(bricks, "space", -1)
    before_plane = split_planes(previous)[1]
    after_plane = split_planes(following)[0]
    return (before_plane, after_plane)


def spread(own_part):
    entire = lax.all_gather(own_part, "chan", axis=2, tiled=True)
    before_plane, after_plane = neighbour_planes(entire)
    return (entire, before_plane, after_plane)


def assemble(entire, before_plane, after_plane, table, own_start):
    brick_count, depth = (entire.shape[0], entire.shape[1])
    lists, order = piece_tables()
    sources = (
        jnp.concatenate([before_plane, jnp.zeros((1, depth, 64), entire.dtype)], axis=0),
        jnp.concatenate([entire, jnp.zeros((1, depth, 512), entire.dtype)], axis=0),
        jnp.concatenate([after_plane, jnp.zeros((1, depth, 64), entire.dtype)], axis=0),
    )
    pieces = []
    for step_x in range(3):
        block_start = own_start + (step_x - 1) * brick_count
        for step_y in range(3):
            for step_z in range(3):
                index_k = 9 * step_x + 3 * step_y + step_z
                listed = table[:, index_k]
                local_ids = jnp.where(listed < 0, brick_count, listed - block_start)
                picked = jnp.take(sources[step_x], local_ids, axis=0)
                pieces.append(jnp.take(picked, jnp.asarray(lists[index_k]), axis=2))
    joined = jnp.concatenate(pieces, axis=2)
    flat = jnp.take(joined, jnp.asarray(order), axis=2)
    return jnp.pad(flat, ((0, 0), (0, 0), (0, source_width - 1000)))


def to_padded_grid(bricks):
    into_grid, valid, back_ids = grid_tables()
    taken = jnp.take(bricks, jnp.asarray(into_grid), axis=2)
    return taken * jnp.asarray(valid).astype(bricks.dtype)


def from_padded_grid(flat):
    into_grid, valid, back_ids = grid_tables()
    return jnp.take(flat, jnp.asarray(back_ids), axis=2)


def body(features, weight, cotangent, neighbours):
    brick_count, narrow = (features.shape[0], features.shape[1])
    own_start = lax.axis_index("space") * brick_count
    feat_views = tuple((view[0] for view in spread(features[None])))
    grad_views = tuple((view[0] for view in spread(cotangent[None])))
    padded = assemble(feat_views[0], feat_views[1], feat_views[2], neighbours, own_start)
    grad_flat = to_padded_grid(cotangent)
    running = jnp.zeros((brick_count, narrow, flat_width), jnp.float32)
    kernel_terms = []
    for step_x in range(3):
        for step_y in range(3):
            for step_z in range(3):
                index_k = 9 * step_x + 3 * step_y + step_z
                offset = 100 * step_x + 10 * step_y + step_z
                window = padded[:, :, offset : offset + flat_width]
                running = running + jnp.einsum(
                    "oc,rcn->ron", weight[index_k], window, preferred_element_type=jnp.float32
                )
                kernel_terms.append(
                    jnp.einsum("ron,rcn->oc", grad_flat, window, preferred_element_type=jnp.float32)
                )
    output = from_padded_grid(running).astype(jnp.bfloat16)
    voxel_total = brick_count * lax.axis_size("space") * 512
    summed = lax.psum(jnp.stack(kernel_terms), "space")
    grad_weight = summed * voxel_total ** (-0.5)
    full_kernel = lax.all_gather(weight, "chan", axis=1, tiled=True)
    column_start = lax.axis_index("chan") * narrow
    my_kernel = lax.dynamic_slice_in_dim(full_kernel, column_start, narrow, 2)
    grad_padded = assemble(grad_views[0], grad_views[1], grad_views[2], neighbours, own_start)
    backward = jnp.zeros((brick_count, narrow, flat_width), jnp.float32)
    for step_x in range(3):
        for step_y in range(3):
            for step_z in range(3):
                index_k = 9 * step_x + 3 * step_y + step_z
                offset = 100 * step_x + 10 * step_y + step_z
                window = grad_padded[:, :, offset : offset + flat_width]
                backward = backward + jnp.einsum(
                    "oc,ron->rcn",
                    my_kernel[26 - index_k],
                    window,
                    preferred_element_type=jnp.float32,
                )
    grad_input = from_padded_grid(backward).astype(jnp.bfloat16)
    return (output, grad_input, grad_weight)


def solution(mesh):
    in_specs = (
        P("space", "chan", None),
        P(None, "chan", None),
        P("space", "chan", None),
        P("space", None),
    )
    out_specs = (P("space", "chan", None), P("space", "chan", None), P(None, "chan", None))
    return jax.shard_map(body, mesh=mesh, in_specs=in_specs, out_specs=out_specs, check_vma=False)
```

profile of v0, /device:TPU:2, one launch (start us, length us, event | category | flops | bytes accessed | tf_op | source)
XLA Modules:
  0.0 693.8 jit_solution(12567140329959811649)
XLA Ops:
  7.2 15.1 %all-gather = bf16[8,64,512]{2,1,0:T(8,128)(2,1)} all-gather(bf16[8,16,512]{2,1,0:T(8,128)(2,1)} %param.84), channel_id=2, replica_groups=mesh['space'=128,'chan'=4] {'chan'}, dimensions={1}, use_global_device_ids=true | all-gather | bytes 655360 | tf_op jit(solution)/shard_map/all_gather | solution.py:72
  22.4 1.9 collective-permute-start
  24.3 3.6 collective-permute-start.1
  27.9 13.7 %all-gather.1 = bf16[8,64,512]{2,1,0:T(8,128)(2,1)} all-gather(bf16[8,16,512]{2,1,0:T(8,128)(2,1)} %param.86), channel_id=3, replica_groups=mesh['space'=128,'chan'=4] {'chan'}, dimensions={1}, use_global_device_ids=true | all-gather | bytes 655360 | tf_op jit(solution)/shard_map/all_gather | solution.py:72
  41.7 1.9 collective-permute-start.2
  43.6 4.2 collective-permute-start.3
  99.5 1.8 gather_fusion.16
  103.8 2.5 gather_fusion.18
  111.6 2.5 gather_fusion.22
  117.1 2.0 gather_fusion.24
  119.1 2.4 gather_fusion.72
  126.3 2.5 gather_fusion.26
  128.8 2.5 gather_fusion.74
  143.3 2.5 gather_fusion.30
  145.9 2.5 gather_fusion.78
  156.0 4.0 gather_fusion
  160.0 4.5 multiply_bitcast_fusion
  167.5 14.2 %all_gather.11 = bf16[27,64,64]{2,1,0:T(8,128)(2,1)} all-gather(bf16[27,16,64]{2,1,0:T(8,128)(2,1)S(1)} %copy-done.25), channel_id=1, replica_groups=mesh['space'=128,'chan'=4] {'chan'}, dimensions={1}, use_global_device_ids=true | all-gather | bytes 276480 | tf_op jit(solution)/shard_map/all_gather | solution.py:136
  229.4 1.8 broadcast_select_fusion.34
  249.1 2.2 gather_fusion.8
  251.3 2.2 gather_fusion.56
  259.9 1.9 slice_select_fusion.1
  308.1 2.6 bitcast_dynamic-update-slice_fusion
  322.2 5.1 gather_fusion.47
  327.3 2.1 copy.219
  346.1 9.2 %gather_fusion.95 = bf16[1000,8,64]{2,1,0:T(8,128)(2,1)} fusion(bf16[8,64,1000]{1,0,2:T(8,128)(2,1)} %get-tuple-element.60, s32[1024]{0:T(1024)S(1)} %get-tuple-element.187), kind=kCustom, calls=%fused_computation.94.clone | custom fusion | bytes 2052000 | tf_op jit(solution)/shard_map/jit(_take)/gather | solution.py:96
  355.4 2.7 copy.248
  382.6 1.9 copy.250
  384.5 1.8 gather_fusion.96
  387.7 1.9 copy.220
  389.6 1.8 gather_fusion.48
  392.8 292.1 %all-reduce.10.cloned.1.call-done = f32[27,16,64]{2,1,0:T(8,128)} async-done(((f32[27,16,64]{2,1,0:T(8,128)}), f32[27,16,64]{2,1,0:T(8,128)}) %all-reduce.10.cloned.1.call-update) | async-done | bytes 110608 | tf_op jit(solution)/shard_map/psum | solution.py:134
  (526 shorter events, 264.0 us)
Async XLA Ops:
  7.2 46.5 %copy-start = (s32[8,27]{1,0:T(8,128)S(1)}, s32[8,27]{1,0:T(8,128)}, u32[]{:S(2)}) copy-start(s32[8,27]{1,0:T(8,128)} %param.87) | copy-start | bytes 2596
  7.2 677.7 %all-reduce.10.cloned.1.call-start = ((), (), s32[]{:S(2)}) async-start(), calls=%async_computation | async-start | bytes 442368 | tf_op jit(solution)/shard_map/psum | solution.py:134
  22.4 160.4 %collective-permute-start = (bf16[1,8,64,512]{3,2,1,0:T(8,128)(2,1)}, bf16[1,8,64,512]{3,2,1,0:T(8,128)(2,1)}, u32[]{:S(2)}, u32[]{:S(2)}) collective-permute-start(bf16[1,8,64,512]{3,2,1,0:T(8,128)(2,1)} %bitcast), channel_id=1, source_target_pairs={{0,4},{4,8},{8,12},{12,16},{16,20},{20,24},{24,28},{28,32},{32,36}... | collective-permute-start | bytes 1572872 | tf_op jit(solution)/shard_map/ppermute | solution.py:14
  24.3 179.5 %collective-permute-start.1 = (bf16[1,8,64,512]{3,2,1,0:T(8,128)(2,1)}, bf16[1,8,64,512]{3,2,1,0:T(8,128)(2,1)}, u32[]{:S(2)}, u32[]{:S(2)}) collective-permute-start(bf16[1,8,64,512]{3,2,1,0:T(8,128)(2,1)} %bitcast), channel_id=1, source_target_pairs={{4,0},{8,4},{12,8},{16,12},{20,16},{24,20},{28,24},{32,28},{36,32}... | collective-permute-start | bytes 1572872 | tf_op jit(solution)/shard_map/ppermute | solution.py:14
  41.7 140.0 %collective-permute-start.2 = (bf16[1,8,64,512]{3,2,1,0:T(8,128)(2,1)}, bf16[1,8,64,512]{3,2,1,0:T(8,128)(2,1)}, u32[]{:S(2)}, u32[]{:S(2)}) collective-permute-start(bf16[1,8,64,512]{3,2,1,0:T(8,128)(2,1)} %bitcast.89), channel_id=1, source_target_pairs={{0,4},{4,8},{8,12},{12,16},{16,20},{20,24},{24,28},{28,32},{32,36}... | collective-permute-start | bytes 1572872 | tf_op jit(solution)/shard_map/ppermute | solution.py:14
  43.6 161.2 %collective-permute-start.3 = (bf16[1,8,64,512]{3,2,1,0:T(8,128)(2,1)}, bf16[1,8,64,512]{3,2,1,0:T(8,128)(2,1)}, u32[]{:S(2)}, u32[]{:S(2)}) collective-permute-start(bf16[1,8,64,512]{3,2,1,0:T(8,128)(2,1)} %bitcast.89), channel_id=1, source_target_pairs={{4,0},{8,4},{12,8},{16,12},{20,16},{24,20},{28,24},{32,28},{36,32}... | collective-permute-start | bytes 1572872 | tf_op jit(solution)/shard_map/ppermute | solution.py:14
  50.4 35.4 %copy-start.41 = (s32[8]{0:T(128)}, s32[8]{0:T(128)S(1)}, u32[]{:S(2)}) copy-start(s32[8]{0:T(128)S(1)} %get-tuple-element.53) | copy-start | bytes 100
  54.1 99.3 %copy-start.59 = (s32[8]{0:T(128)}, s32[8]{0:T(128)S(1)}, u32[]{:S(2)}) copy-start(s32[8]{0:T(128)S(1)} %get-tuple-element.40) | copy-start | bytes 100
  136.3 12.0 %copy-start.2 = (bf16[8,64,512]{2,1,0:T(8,128)(2,1)S(1)}, bf16[8,64,512]{2,1,0:T(8,128)(2,1)}, u32[]{:S(2)}) copy-start(bf16[8,64,512]{2,1,0:T(8,128)(2,1)} %gather_fusion.31) | copy-start | bytes 1572868
  136.3 12.0 %copy-start.3 = (bf16[8,64,512]{2,1,0:T(8,128)(2,1)S(1)}, bf16[8,64,512]{2,1,0:T(8,128)(2,1)}, u32[]{:S(2)}) copy-start(bf16[8,64,512]{2,1,0:T(8,128)(2,1)} %gather_fusion.79) | copy-start | bytes 1572868
  148.6 11.4 %copy-start.30 = (bf16[896]{0:T(1024)(128)(2,1)S(1)}, bf16[896]{0:T(1024)(128)(2,1)}, u32[]{:S(2)}) copy-start(bf16[896]{0:T(1024)(128)(2,1)} %constant.267) | copy-start | bytes 5380
  208.4 14.8 %copy-start.48 = (pred[8]{0:T(512)(128)(4,1)S(1)}, pred[8]{0:T(512)(128)(4,1)}, u32[]{:S(2)}) copy-start(pred[8]{0:T(512)(128)(4,1)} %get-tuple-element.184) | copy-start | bytes 28
  211.9 13.1 %copy-start.46 = (pred[8]{0:T(512)(128)(4,1)S(1)}, pred[8]{0:T(512)(128)(4,1)}, u32[]{:S(2)}) copy-start(pred[8]{0:T(512)(128)(4,1)} %get-tuple-element.185) | copy-start | bytes 28
  214.5 13.0 %copy-start.47 = (pred[8]{0:T(512)(128)(4,1)S(1)}, pred[8]{0:T(512)(128)(4,1)}, u32[]{:S(2)}) copy-start(pred[8]{0:T(512)(128)(4,1)} %get-tuple-element.183) | copy-start | bytes 28
  215.9 13.5 %copy-start.45 = (pred[8]{0:T(512)(128)(4,1)S(1)}, pred[8]{0:T(512)(128)(4,1)}, u32[]{:S(2)}) copy-start(pred[8]{0:T(512)(128)(4,1)} %get-tuple-element.182) | copy-start | bytes 28
  225.0 19.0 %copy-start.44 = (pred[8]{0:T(512)(128)(4,1)S(1)}, pred[8]{0:T(512)(128)(4,1)}, u32[]{:S(2)}) copy-start(pred[8]{0:T(512)(128)(4,1)} %get-tuple-element.181) | copy-start | bytes 28
  229.4 24.0 %copy-start.20 = (bf16[8,64,64]{2,1,0:T(8,128)(2,1)S(1)}, bf16[8,64,64]{2,1,0:T(8,128)(2,1)}, u32[]{:S(2)}) copy-start(bf16[8,64,64]{2,1,0:T(8,128)(2,1)} %gather_fusion.9) | copy-start | bytes 196612
  229.4 24.0 %copy-start.43 = (pred[8]{0:T(512)(128)(4,1)S(1)}, pred[8]{0:T(512)(128)(4,1)}, u32[]{:S(2)}) copy-start(pred[8]{0:T(512)(128)(4,1)} %get-tuple-element.180) | copy-start | bytes 28
  242.4 21.4 %copy-start.19 = (bf16[8,64,64]{2,1,0:T(8,128)(2,1)S(1)}, bf16[8,64,64]{2,1,0:T(8,128)(2,1)}, u32[]{:S(2)}) copy-start(bf16[8,64,64]{2,1,0:T(8,128)(2,1)} %gather_fusion.60) | copy-start | bytes 196612
  242.4 21.4 %copy-start.35 = (pred[8]{0:T(512)(128)(4,1)S(1)}, pred[8]{0:T(512)(128)(4,1)}, u32[]{:S(2)}) copy-start(pred[8]{0:T(512)(128)(4,1)} %get-tuple-element.177) | copy-start | bytes 28
  251.2 18.1 %copy-start.34 = (pred[8]{0:T(512)(128)(4,1)S(1)}, pred[8]{0:T(512)(128)(4,1)}, u32[]{:S(2)}) copy-start(pred[8]{0:T(512)(128)(4,1)} %get-tuple-element.176) | copy-start | bytes 28
  259.9 13.8 %copy-start.18 = (bf16[8,64,64]{2,1,0:T(8,128)(2,1)S(1)}, bf16[8,64,64]{2,1,0:T(8,128)(2,1)}, u32[]{:S(2)}) copy-start(bf16[8,64,64]{2,1,0:T(8,128)(2,1)} %gather_fusion.82) | copy-start | bytes 196612
  259.9 13.7 %copy-start.40 = (pred[8]{0:T(512)(128)(4,1)S(1)}, pred[8]{0:T(512)(128)(4,1)}, u32[]{:S(2)}) copy-start(pred[8]{0:T(512)(128)(4,1)} %get-tuple-element.165) | copy-start | bytes 28
  281.5 13.3 %copy-start.16 = (bf16[64,8,64]{2,1,0:T(8,128)(2,1)S(1)}, bf16[64,8,64]{2,1,0:T(8,128)(2,1)}, u32[]{:S(2)}) copy-start(bf16[64,8,64]{2,1,0:T(8,128)(2,1)} %gather_fusion.8) | copy-start | bytes 196612
  281.5 13.3 %copy-start.17 = (bf16[64,8,64]{2,1,0:T(8,128)(2,1)S(1)}, bf16[64,8,64]{2,1,0:T(8,128)(2,1)}, u32[]{:S(2)}) copy-start(bf16[64,8,64]{2,1,0:T(8,128)(2,1)} %gather_fusion.56) | copy-start | bytes 196612
  281.5 13.2 %copy-start.31 = (pred[64]{0:T(512)(128)(4,1)S(1)}, pred[64]{0:T(512)(128)(4,1)}, u32[]{:S(2)}) copy-start(pred[64]{0:T(512)(128)(4,1)} %broadcast_compare_fusion.2) | copy-start | bytes 196
  281.6 13.9 %copy-start.33 = (pred[8]{0:T(512)(128)(4,1)S(1)}, pred[8]{0:T(512)(128)(4,1)}, u32[]{:S(2)}) copy-start(pred[8]{0:T(512)(128)(4,1)} %get-tuple-element.179) | copy-start | bytes 28
  281.6 15.8 %copy-start.32 = (pred[8]{0:T(512)(128)(4,1)S(1)}, pred[8]{0:T(512)(128)(4,1)}, u32[]{:S(2)}) copy-start(pred[8]{0:T(512)(128)(4,1)} %broadcast_compare_fusion.1) | copy-start | bytes 28
  284.0 24.0 %copy-start.1 = (bf16[512,8,64]{2,1,0:T(8,128)(2,1)S(1)}, bf16[512,8,64]{2,1,0:T(8,128)(2,1)}, u32[]{:S(2)}) copy-start(bf16[512,8,64]{2,1,0:T(8,128)(2,1)} %gather_fusion.72) | copy-start | bytes 1572868
  284.0 24.0 %copy-start.57 = (pred[512]{0:T(512)(128)(4,1)S(1)}, pred[512]{0:T(512)(128)(4,1)}, u32[]{:S(2)}) copy-start(pred[512]{0:T(512)(128)(4,1)} %broadcast_compare_fusion) | copy-start | bytes 1540
  308.1 12.1 %copy-start.51 = (pred[8]{0:T(512)(128)(4,1)S(1)}, pred[8]{0:T(512)(128)(4,1)}, u32[]{:S(2)}) copy-start(pred[8]{0:T(512)(128)(4,1)} %get-tuple-element.160) | copy-start | bytes 28
  308.1 13.4 %copy-start.50 = (pred[8]{0:T(512)(128)(4,1)S(1)}, pred[8]{0:T(512)(128)(4,1)}, u32[]{:S(2)}) copy-start(pred[8]{0:T(512)(128)(4,1)} %get-tuple-element.158) | copy-start | bytes 28
  (45 other events, 259.4 us)
Sparse Core Ops, SparseCore 0:
  346.3 338.5 all-reduce.9
where the time goes:
time: 703 us; the launch traced here: 694 us
  waiting for transfers between devices  292 us (42%)
  local copies, waits for them, and re-layouts  236 us (34%)
  other arithmetic  54.3 us (8%)
  blocking collectives  43.1 us (6%)
  matrix products  40.2 us (6%)
  between operations  16.1 us (2%)
  starting transfers between devices  11.7 us (2%)
    psum x1, waiting for transfers between devices, body(): summed = lax.psum(jnp.stack(kernel_terms), 'space')  292 us
    gather x54, local copies, waits for them, and re-layouts, assemble(): picked = jnp.take(sources[step_x], local_ids, axis=0)  60.5 us
    gather x38, local copies, waits for them, and re-layouts, assemble(): pieces.append(jnp.take(picked, jnp.asarray(lists[index_k]), axis=2))  54.5 us
    select_n x38, local copies, waits for them, and re-layouts, assemble(): picked = jnp.take(sources[step_x], local_ids, axis=0)  42.1 us
    unnamed x183, local copies, waits for them, and re-layouts  30.2 us
    all_gather x2, blocking collectives, spread(): entire = lax.all_gather(own_part, 'chan', axis=2, tiled=True)  28.9 us
    select_n x38, other arithmetic, assemble(): picked = jnp.take(sources[step_x], local_ids, axis=0)  23.9 us
    gather x4, local copies, waits for them, and re-layouts, assemble(): flat = jnp.take(joined, jnp.asarray(order), axis=2)  19.1 us
  transfers between devices with their start and end apart: 5, of which 1 were waited for; matrix products, arithmetic and copies ran while one was open for 27% of the time, Pallas kernels for 0%

commit v1 on v0

--- a/solution.py
+++ b/solution.py
@@ -69,7 +69,9 @@
 
 
 def spread(own_part):
-    entire = lax.all_gather(own_part, "chan", axis=2, tiled=True)
+    entire = jnp.concatenate(
+        lax.all_to_all(jnp.stack([own_part] * lax.axis_size("chan")), "chan", 0, 0), axis=2
+    )
     before_plane, after_plane = neighbour_planes(entire)
     return (entire, before_plane, after_plane)
 

time: 703 us -> 775 us (1.10)
  local copies, waits for them, and re-layouts: 236 us -> 294 us
  blocking collectives: 43.1 us -> 14.2 us
  other arithmetic: 54.3 us -> 82.4 us
  starting transfers between devices: 11.7 us -> 21.6 us
    all_gather x2 -> x0, blocking collectives: 28.9 us -> none  [spread(): entire = lax.all_gather(own_part, 'chan', axis=2, tiled=True)]
    select_n x38, local copies, waits for them, and re-layouts: 42.1 us -> 66.8 us  [assemble(): picked = jnp.take(sources[step_x], local_ids, axis=0)]
    gather x38, local copies, waits for them, and re-layouts: 54.5 us -> 70 us  [assemble(): pieces.append(jnp.take(picked, jnp.asarray(lists[index_k]), axis=2))]
    gather x36, other arithmetic: 2.57 us -> 16.2 us
    select_n x38, other arithmetic: 23.9 us -> 34.4 us  [assemble(): picked = jnp.take(sources[step_x], local_ids, axis=0)]
    all_to_all x0 -> x2, starting transfers between devices: none -> 8.56 us  [spread(): lax.all_to_all(jnp.stack([own_part] * lax.axis_size('chan')), 'chan', 0, 0)]
    unnamed x183 -> x197, local copies, waits for them, and re-layouts: 30.2 us -> 34.4 us
  transfers between devices with their start and end apart: 5 -> 7, of which waited for: 1 -> 2; matrix products, arithmetic and copies ran while one was open for 27% -> 27% of each run, Pallas kernels for 0% -> 0%
where the time goes in v1:
time: 775 us; the launch traced here: 766 us
  waiting for transfers between devices  298 us (38%)
  local copies, waits for them, and re-layouts  294 us (38%)
  other arithmetic  82.4 us (11%)
  matrix products  40.2 us (5%)
  starting transfers between devices  21.6 us (3%)
  between operations  15.4 us (2%)
  blocking collectives  14.2 us (2%)
    psum x1, waiting for transfers between devices, body(): summed = lax.psum(jnp.stack(kernel_terms), 'space')  291 us
    gather x38, local copies, waits for them, and re-layouts, assemble(): pieces.append(jnp.take(picked, jnp.asarray(lists[index_k]), axis=2))  70 us
    gather x54, local copies, waits for them, and re-layouts, assemble(): picked = jnp.take(sources[step_x], local_ids, axis=0)  68.1 us
    select_n x38, local copies, waits for them, and re-layouts, assemble(): picked = jnp.take(sources[step_x], local_ids, axis=0)  66.8 us
    select_n x38, other arithmetic, assemble(): picked = jnp.take(sources[step_x], local_ids, axis=0)  34.4 us
    unnamed x197, local copies, waits for them, and re-layouts  34.4 us
    gather x4, local copies, waits for them, and re-layouts, assemble(): flat = jnp.take(joined, jnp.asarray(order), axis=2)  19 us
    select_n x14, local copies, waits for them, and re-layouts, assemble(): pieces.append(jnp.take(picked, jnp.asarray(lists[index_k]), axis=2))  16.5 us
  transfers between devices with their start and end apart: 7, of which 2 were waited for; matrix products, arithmetic and copies ran while one was open for 27% of the time, Pallas kernels for 0%

profile of v1, /device:TPU:2, one launch (start us, length us, event | category | flops | bytes accessed | tf_op | source)
XLA Modules:
  0.0 766.0 jit_solution(17260468396241331615)
XLA Ops:
  9.0 4.5 all-to-all-start
  39.9 3.6 gather_fusion
  43.5 4.5 multiply_bitcast_fusion
  49.8 14.2 %all_gather.3 = bf16[27,64,64]{2,1,0:T(8,128)(2,1)} all-gather(bf16[27,16,64]{2,1,0:T(8,128)(2,1)S(1)} %copy-done.32), channel_id=1, replica_groups=mesh['space'=128,'chan'=4] {'chan'}, dimensions={1}, use_global_device_ids=true | all-gather | bytes 276480 | tf_op jit(solution)/shard_map/all_gather | solution.py:138
  68.5 4.1 all-to-all-start.1
  73.9 6.8 all-to-all-done.1
  104.2 3.6 collective-permute-start.1
  109.7 5.4 collective-permute-start.3
  115.2 2.4 broadcast_select_fusion.16
  128.5 2.3 broadcast_select_fusion
  132.5 2.8 copy.199
  135.3 2.7 copy.200
  138.1 2.8 copy.201
  148.1 2.6 gather_fusion.18
  150.8 2.6 gather_fusion.66
  160.7 2.6 gather_fusion.22
  163.3 2.6 gather_fusion.70
  171.3 2.8 copy.203
  174.1 2.8 copy.233
  176.9 2.7 gather_fusion.26
  179.6 2.6 gather_fusion.74
  183.9 2.8 copy.205
  194.0 2.6 gather_fusion.30
  196.6 2.6 gather_fusion.78
  199.2 2.8 copy.206
  282.0 2.2 gather_fusion.8
  284.2 2.2 gather_fusion.56
  381.4 3.1 bitcast_dynamic-update-slice_fusion
  395.8 5.1 gather_fusion.47
  419.7 9.2 %gather_fusion.95 = bf16[1000,8,64]{2,1,0:T(8,128)(2,1)} fusion(bf16[8,64,1000]{1,0,2:T(8,128)(2,1)} %get-tuple-element.60, s32[1024]{0:T(1024)S(1)} %get-tuple-element.187), kind=kCustom, calls=%fused_computation.94.clone | custom fusion | bytes 2052000 | tf_op jit(solution)/shard_map/jit(_take)/gather | solution.py:98
  428.9 2.7 copy.250
  466.3 291.1 %all-reduce.10.cloned.1.call-done = f32[27,16,64]{2,1,0:T(8,128)} async-done(((f32[27,16,64]{2,1,0:T(8,128)}), f32[27,16,64]{2,1,0:T(8,128)}) %all-reduce.10.cloned.1.call-update) | async-done | bytes 110608 | tf_op jit(solution)/shard_map/psum | solution.py:136
  (546 shorter events, 343.1 us)
Async XLA Ops:
  7.2 32.7 %copy-start.36 = (s32[896]{0:T(1024)S(1)}, s32[896]{0:T(1024)}, u32[]{:S(2)}) copy-start(s32[896]{0:T(1024)} %constant.605) | copy-start | bytes 10756
  7.2 32.7 %copy-start.37 = (s32[1000]{0:T(1024)S(1)}, s32[1000]{0:T(1024)}, u32[]{:S(2)}) copy-start(s32[1000]{0:T(1024)} %constant.640) | copy-start | bytes 12004
  7.2 36.3 %copy-start.38 = (bf16[896]{0:T(1024)(128)(2,1)S(1)}, bf16[896]{0:T(1024)(128)(2,1)}, u32[]{:S(2)}) copy-start(bf16[896]{0:T(1024)(128)(2,1)} %constant.267) | copy-start | bytes 5380
  7.2 31.8 %copy-start.23 = (bf16[8,16,512]{2,1,0:T(8,128)(2,1)S(1)}, bf16[8,16,512]{2,1,0:T(8,128)(2,1)}, u32[]{:S(2)}) copy-start(bf16[8,16,512]{2,1,0:T(8,128)(2,1)} %param.86) | copy-start | bytes 393220
  9.0 58.6 %all-to-all-start = ((bf16[4,1,8,16,512]{4,3,2,1,0:T(8,128)(2,1)}), bf16[4,1,8,16,512]{4,3,2,1,0:T(8,128)(2,1)S(1)}, u32[]{:S(2)}, u32[]{:S(2)}) async-start(bf16[4,1,8,16,512]{4,3,2,1,0:T(8,128)(2,1)} %stack.90), calls=%async_computation | async-start | bytes 1048576 | tf_op jit(solution)/shard_map/all_to_all | solution.py:73
  28.9 55.4 %copy-start.35 = (s32[1024]{0:T(1024)}, s32[1024]{0:T(1024)S(1)}, u32[]{:S(2)}) copy-start(s32[1024]{0:T(1024)S(1)} %pad_clamp_fusion.27) | copy-start | bytes 12292
  48.0 17.9 %copy-start.72 = (s32[8]{0:T(128)S(1)}, s32[8]{0:T(128)}, u32[]{:S(2)}) copy-start(s32[8]{0:T(128)} %constant.636) | copy-start | bytes 100
  48.0 17.9 %copy-start.73 = (s32[64]{0:T(128)S(1)}, s32[64]{0:T(128)}, u32[]{:S(2)}) copy-start(s32[64]{0:T(128)} %constant.637) | copy-start | bytes 772
  68.5 12.2 %all-to-all-start.1 = ((bf16[4,1,8,16,512]{4,3,2,1,0:T(8,128)(2,1)}), bf16[4,1,8,16,512]{4,3,2,1,0:T(8,128)(2,1)S(1)}, u32[]{:S(2)}, u32[]{:S(2)}) async-start(bf16[4,1,8,16,512]{4,3,2,1,0:T(8,128)(2,1)} %stack.91), calls=%async_computation.1 | async-start | bytes 1048576 | tf_op jit(solution)/shard_map/all_to_all | solution.py:73
  72.6 684.7 %all-reduce.10.cloned.1.call-start = ((), (), s32[]{:S(2)}) async-start(), calls=%async_computation.2 | async-start | bytes 442368 | tf_op jit(solution)/shard_map/psum | solution.py:136
  102.1 106.4 %collective-permute-start = (bf16[1,8,64,512]{3,2,1,0:T(8,128)(2,1)}, bf16[1,8,64,512]{3,2,1,0:T(8,128)(2,1)}, u32[]{:S(2)}, u32[]{:S(2)}) collective-permute-start(bf16[1,8,64,512]{3,2,1,0:T(8,128)(2,1)} %bitcast.677), channel_id=1, source_target_pairs={{0,4},{4,8},{8,12},{12,16},{16,20},{20,24},{24,28},{28,32},{32,36}... | collective-permute-start | bytes 1572872 | tf_op jit(solution)/shard_map/ppermute | solution.py:14
  104.2 128.6 %collective-permute-start.1 = (bf16[1,8,64,512]{3,2,1,0:T(8,128)(2,1)}, bf16[1,8,64,512]{3,2,1,0:T(8,128)(2,1)}, u32[]{:S(2)}, u32[]{:S(2)}) collective-permute-start(bf16[1,8,64,512]{3,2,1,0:T(8,128)(2,1)} %bitcast.678), channel_id=1, source_target_pairs={{4,0},{8,4},{12,8},{16,12},{20,16},{24,20},{28,24},{32,28},{36,32}... | collective-permute-start | bytes 1572872 | tf_op jit(solution)/shard_map/ppermute | solution.py:14
  107.8 99.7 %collective-permute-start.2 = (bf16[1,8,64,512]{3,2,1,0:T(8,128)(2,1)}, bf16[1,8,64,512]{3,2,1,0:T(8,128)(2,1)}, u32[]{:S(2)}, u32[]{:S(2)}) collective-permute-start(bf16[1,8,64,512]{3,2,1,0:T(8,128)(2,1)} %bitcast.680), channel_id=1, source_target_pairs={{0,4},{4,8},{8,12},{12,16},{16,20},{20,24},{24,28},{28,32},{32,36}... | collective-permute-start | bytes 1572872 | tf_op jit(solution)/shard_map/ppermute | solution.py:14
  109.7 123.9 %collective-permute-start.3 = (bf16[1,8,64,512]{3,2,1,0:T(8,128)(2,1)}, bf16[1,8,64,512]{3,2,1,0:T(8,128)(2,1)}, u32[]{:S(2)}, u32[]{:S(2)}) collective-permute-start(bf16[1,8,64,512]{3,2,1,0:T(8,128)(2,1)} %bitcast.681), channel_id=1, source_target_pairs={{4,0},{8,4},{12,8},{16,12},{20,16},{24,20},{28,24},{32,28},{36,32}... | collective-permute-start | bytes 1572872 | tf_op jit(solution)/shard_map/ppermute | solution.py:14
  237.3 18.7 %copy-start.51 = (pred[8]{0:T(512)(128)(4,1)S(1)}, pred[8]{0:T(512)(128)(4,1)}, u32[]{:S(2)}) copy-start(pred[8]{0:T(512)(128)(4,1)} %get-tuple-element.185) | copy-start | bytes 28
  257.9 18.9 %copy-start.47 = (pred[8]{0:T(512)(128)(4,1)S(1)}, pred[8]{0:T(512)(128)(4,1)}, u32[]{:S(2)}) copy-start(pred[8]{0:T(512)(128)(4,1)} %get-tuple-element.182) | copy-start | bytes 28
  262.3 24.0 %copy-start.29 = (bf16[8,64,64]{2,1,0:T(8,128)(2,1)S(1)}, bf16[8,64,64]{2,1,0:T(8,128)(2,1)}, u32[]{:S(2)}) copy-start(bf16[8,64,64]{2,1,0:T(8,128)(2,1)} %gather_fusion.9) | copy-start | bytes 196612
  262.3 24.0 %copy-start.68 = (pred[8]{0:T(512)(128)(4,1)S(1)}, pred[8]{0:T(512)(128)(4,1)}, u32[]{:S(2)}) copy-start(pred[8]{0:T(512)(128)(4,1)} %get-tuple-element.181) | copy-start | bytes 28
  270.6 23.8 %copy-start.45 = (pred[8]{0:T(512)(128)(4,1)S(1)}, pred[8]{0:T(512)(128)(4,1)}, u32[]{:S(2)}) copy-start(pred[8]{0:T(512)(128)(4,1)} %get-tuple-element.179) | copy-start | bytes 28
  275.3 22.9 %copy-start.43 = (pred[8]{0:T(512)(128)(4,1)S(1)}, pred[8]{0:T(512)(128)(4,1)}, u32[]{:S(2)}) copy-start(pred[8]{0:T(512)(128)(4,1)} %get-tuple-element.178) | copy-start | bytes 28
  284.2 22.2 %copy-start.42 = (pred[8]{0:T(512)(128)(4,1)S(1)}, pred[8]{0:T(512)(128)(4,1)}, u32[]{:S(2)}) copy-start(pred[8]{0:T(512)(128)(4,1)} %get-tuple-element.177) | copy-start | bytes 28
  294.4 21.2 %copy-start.48 = (pred[8]{0:T(512)(128)(4,1)S(1)}, pred[8]{0:T(512)(128)(4,1)}, u32[]{:S(2)}) copy-start(pred[8]{0:T(512)(128)(4,1)} %get-tuple-element.165) | copy-start | bytes 28
  304.9 24.2 %copy-start.46 = (pred[8]{0:T(512)(128)(4,1)S(1)}, pred[8]{0:T(512)(128)(4,1)}, u32[]{:S(2)}) copy-start(pred[8]{0:T(512)(128)(4,1)} %get-tuple-element.163) | copy-start | bytes 28
  314.6 22.6 %copy-start.44 = (pred[8]{0:T(512)(128)(4,1)S(1)}, pred[8]{0:T(512)(128)(4,1)}, u32[]{:S(2)}) copy-start(pred[8]{0:T(512)(128)(4,1)} %get-tuple-element.162) | copy-start | bytes 28
  322.2 23.7 %copy-start.53 = (pred[8]{0:T(512)(128)(4,1)S(1)}, pred[8]{0:T(512)(128)(4,1)}, u32[]{:S(2)}) copy-start(pred[8]{0:T(512)(128)(4,1)} %get-tuple-element.161) | copy-start | bytes 28
  335.6 22.8 %copy-start.52 = (pred[8]{0:T(512)(128)(4,1)S(1)}, pred[8]{0:T(512)(128)(4,1)}, u32[]{:S(2)}) copy-start(pred[8]{0:T(512)(128)(4,1)} %get-tuple-element.159) | copy-start | bytes 28
  346.7 21.4 %copy-start.27 = (bf16[64,8,64]{2,1,0:T(8,128)(2,1)S(1)}, bf16[64,8,64]{2,1,0:T(8,128)(2,1)}, u32[]{:S(2)}) copy-start(bf16[64,8,64]{2,1,0:T(8,128)(2,1)} %gather_fusion.8) | copy-start | bytes 196612
  346.7 21.4 %copy-start.28 = (bf16[64,8,64]{2,1,0:T(8,128)(2,1)S(1)}, bf16[64,8,64]{2,1,0:T(8,128)(2,1)}, u32[]{:S(2)}) copy-start(bf16[64,8,64]{2,1,0:T(8,128)(2,1)} %gather_fusion.56) | copy-start | bytes 196612
  346.7 21.4 %copy-start.41 = (pred[64]{0:T(512)(128)(4,1)S(1)}, pred[64]{0:T(512)(128)(4,1)}, u32[]{:S(2)}) copy-start(pred[64]{0:T(512)(128)(4,1)} %broadcast_compare_fusion.2) | copy-start | bytes 196
  348.4 20.5 %copy-start.40 = (pred[8]{0:T(512)(128)(4,1)S(1)}, pred[8]{0:T(512)(128)(4,1)}, u32[]{:S(2)}) copy-start(pred[8]{0:T(512)(128)(4,1)} %get-tuple-element.180) | copy-start | bytes 28
  348.4 22.4 %copy-start.39 = (pred[8]{0:T(512)(128)(4,1)S(1)}, pred[8]{0:T(512)(128)(4,1)}, u32[]{:S(2)}) copy-start(pred[8]{0:T(512)(128)(4,1)} %broadcast_compare_fusion.1) | copy-start | bytes 28
  357.4 23.9 %copy-start.66 = (pred[512]{0:T(512)(128)(4,1)S(1)}, pred[512]{0:T(512)(128)(4,1)}, u32[]{:S(2)}) copy-start(pred[512]{0:T(512)(128)(4,1)} %broadcast_compare_fusion) | copy-start | bytes 1540
  (54 other events, 377.4 us)
Sparse Core Ops, SparseCore 0:
  419.8 337.4 all-reduce.9
